TPU v7x, 32 devices: a whole 2x2x4 slice. The times are simulated.
32 devices in a mesh: dp: 8 (over z, x), ctx: 4 (over y, core).
Axes of the slice: x: 2, y: 2, z: 4, core: 2. Of those that a mesh axis runs over, the one named last changes fastest.
Arguments:
- inputs: bfloat16 [8, 512, 5376], P('dp', 'ctx'), may hold values from -6 to 6
- q_proj: bfloat16 [8, 512, 2048], P('dp', 'ctx'), may hold values from -260 to 260
- k_proj: bfloat16 [8, 512, 1024], P('dp', 'ctx'), may hold values from -260 to 260
- v_proj: bfloat16 [8, 512, 1024], P('dp', 'ctx'), may hold values from -6 to 6
- d_attn: bfloat16 [8, 512, 2048], P('dp', 'ctx'), may hold values from -6 to 6
- positions: int32 [8, 512], P('dp', 'ctx'), may hold values from 0 to 511, as said below
- windows: int32 [8], P('dp'), may hold values from 512 to 1024
- q_gain: float32 [128], replicated, may hold values from 0.7 to 5.5
- k_gain: float32 [128], replicated, may hold values from 0.7 to 5.5
- weight: bfloat16 [5376, 4096], P('dp'), may hold values from -0.078125 to 0.078125
Outputs:
- d_inputs: bfloat16 [8, 512, 5376], P('dp', 'ctx')
- d_weight_t: float32 [4096, 5376], P('ctx', 'dp')
- d_q_gain: float32 [128], replicated
- d_k_gain: float32 [128], replicated
Inputs may be any that keep to these rules, and one draw needn't show every extreme that they name: `positions`: within each sequence a position counts the tokens since its document began: it grows by one from token to token and falls to 0 where a document begins; the first token of a sequence has position 0. Some sequence holds a single document.
All inputs are finite; a program needn't handle non-finite values.
Results may differ from a plain program's by a relative error of at most 0.029.
Values may be sent and summed in bfloat16 or wider, within the bound.
A program may use at most 128 MiB of HBM per device.

v0:
```python
import math
import jax
import jax.numpy as jnp
from jax import lax
from jax.sharding import PartitionSpec as P

REACH = 8
score_scale = 168.0 ** (-0.5)
rope_base = 10000.0
norm_eps = 1e-06


def from_behind(value, axis, steps):
    count = lax.axis_size(axis)
    initial, last = (max(0, -steps), min(count, count - steps))
    return lax.ppermute(value, axis, [(source, source + steps) for source in range(initial, last)])


def rotated_unit(projected_rows, gain_vector, token_pos, head_count):
    head_width = gain_vector.shape[0]
    rows_heads = projected_rows.reshape(projected_rows.shape[0], head_count, head_width)
    inverse = lax.rsqrt(jnp.mean(rows_heads * rows_heads, axis=-1, keepdims=True) + norm_eps)
    normed = rows_heads * inverse * gain_vector
    half_width = head_width // 2
    frequency = jnp.exp(
        jnp.arange(half_width, dtype=jnp.float32) * (-2.0 * math.log(rope_base) / head_width)
    )
    angles = token_pos.astype(jnp.float32)[:, None] * frequency[None, :]
    cosine_table = jnp.cos(angles)[:, None, :]
    sine_table = jnp.sin(angles)[:, None, :]
    first_half = normed[..., :half_width]
    second_half = normed[..., half_width:]
    return jnp.concatenate(
        [
            first_half * cosine_table - second_half * sine_table,
            second_half * cosine_table + first_half * sine_table,
        ],
        axis=-1,
    )


def shards(inputs, q_proj, k_proj, v_proj, d_attn, positions, windows, q_gain, k_gain, weight):
    tok_rows = inputs.shape[1]
    head_width = q_gain.shape[0]
    query_heads = q_proj.shape[2] // head_width
    key_heads = k_proj.shape[2] // head_width
    group_size = query_heads // key_heads
    token_pos = positions[0]
    window = windows[0]
    input_cols = lax.all_to_all(inputs, "dp", split_axis=2, concat_axis=0, tiled=True)

    def query_side(projected_rows, gain_vector):
        return rotated_unit(projected_rows, gain_vector, token_pos, query_heads)

    def key_side(projected_rows, gain_vector):
        return rotated_unit(projected_rows, gain_vector, token_pos, key_heads)

    q_full, query_back = jax.vjp(query_side, q_proj[0].astype(jnp.float32), q_gain)
    k_full, key_back = jax.vjp(key_side, k_proj[0].astype(jnp.float32), k_gain)
    query_rotated = q_full.astype(jnp.bfloat16).reshape(tok_rows, key_heads, group_size, head_width)
    key_rotated = k_full.astype(jnp.bfloat16)
    v_own = v_proj[0].reshape(tok_rows, key_heads, head_width)
    reach_count = min(REACH, lax.axis_size("ctx") - 1)
    key_blocks = [key_rotated]
    value_blocks = [v_own]
    for distance_steps in range(1, reach_count + 1):
        far_keys, far_values = from_behind((key_rotated, v_own), "ctx", distance_steps)
        key_blocks.append(far_keys)
        value_blocks.append(far_values)
    all_keys = jnp.stack(key_blocks)
    all_values = jnp.stack(value_blocks)
    block_ids = jnp.arange(reach_count + 1, dtype=jnp.int32)
    offsets = jnp.arange(tok_rows, dtype=jnp.int32)
    distance = block_ids[None, :, None] * tok_rows + offsets[:, None, None] - offsets[None, None, :]
    allowed = (distance >= 0) & (distance < window) & (distance <= token_pos[:, None, None])
    scores = (
        jnp.einsum("ahgd,bchd->hgabc", query_rotated, all_keys, preferred_element_type=jnp.float32)
        * score_scale
    )
    scores = jnp.where(allowed, scores, -jnp.inf)
    row_max = jnp.max(scores, axis=(3, 4), keepdims=True)
    exponent = jnp.exp(scores - row_max)
    probs = exponent / jnp.sum(exponent, axis=(3, 4), keepdims=True)
    head_gradient = d_attn[0].reshape(tok_rows, key_heads, group_size, head_width)
    dprobs = jnp.einsum(
        "ahgd,bchd->hgabc", head_gradient, all_values, preferred_element_type=jnp.float32
    )
    delta = jnp.sum(probs * dprobs, axis=(3, 4), keepdims=True)
    dscores = (probs * (dprobs - delta)).astype(jnp.bfloat16)
    probs_low = probs.astype(jnp.bfloat16)
    dq_rot = (
        jnp.einsum("hgabc,bchd->ahgd", dscores, all_keys, preferred_element_type=jnp.float32)
        * score_scale
    )
    dk_blocks = (
        jnp.einsum("hgabc,ahgd->bchd", dscores, query_rotated, preferred_element_type=jnp.float32)
        * score_scale
    )
    dv_blocks = jnp.einsum(
        "hgabc,ahgd->bchd", probs_low, head_gradient, preferred_element_type=jnp.float32
    )
    dk_total = dk_blocks[0]
    dv_total = dv_blocks[0]
    for distance_steps in range(1, reach_count + 1):
        back_keys, back_values = from_behind(
            (
                dk_blocks[distance_steps].astype(jnp.bfloat16),
                dv_blocks[distance_steps].astype(jnp.bfloat16),
            ),
            "ctx",
            -distance_steps,
        )
        dk_total = dk_total + back_keys.astype(jnp.float32)
        dv_total = dv_total + back_values.astype(jnp.float32)
    dq_proj, dq_gain = query_back(dq_rot.reshape(tok_rows, query_heads, head_width))
    dk_proj, dk_gain = key_back(dk_total)
    dq_gain_all, dk_gain_all = lax.psum((dq_gain, dk_gain), ("dp", "ctx"))
    dv_proj = dv_total.reshape(tok_rows, key_heads * head_width)
    d_proj = jnp.concatenate([dq_proj, dk_proj, dv_proj], axis=-1).astype(jnp.bfloat16)[None]
    gathered = lax.all_gather(d_proj, "dp", axis=0, tiled=True)
    d_cols = jnp.einsum("btp,dp->btd", gathered, weight, preferred_element_type=jnp.float32)
    d_inputs = lax.all_to_all(
        d_cols.astype(jnp.bfloat16), "dp", split_axis=0, concat_axis=2, tiled=True
    )
    d_weight_t = lax.psum_scatter(
        jnp.einsum("btp,btd->pd", gathered, input_cols, preferred_element_type=jnp.float32).astype(
            jnp.bfloat16
        ),
        "ctx",
        scatter_dimension=0,
        tiled=True,
    ).astype(jnp.float32)
    return (d_inputs, d_weight_t, dq_gain_all, dk_gain_all)


def solution(mesh):
    placed = (
        P("dp", "ctx", None),
        P("dp", "ctx", None),
        P("dp", "ctx", None),
        P("dp", "ctx", None),
        P("dp", "ctx", None),
        P("dp", "ctx"),
        P("dp"),
        P(),
        P(),
        P("dp", None),
    )
    return jax.shard_map(
        shards,
        mesh=mesh,
        in_specs=placed,
        out_specs=(P("dp", "ctx", None), P("ctx", "dp"), P(), P()),
        check_vma=False,
    )
```

profile of v0, /device:TPU:0, one launch (start us, length us, event | category | flops | bytes accessed | tf_op | source)
XLA Modules:
  0.0 321.0 jit_solution(8718791477971543858)
XLA Ops:
  7.2 1.2 copy.176
  8.7 0.7 bitcast_convert_fusion.1
  9.4 0.3 multiply_cosine_fusion
  9.7 0.9 multiply_multiply_fusion.1
  10.6 0.3 subtract_convert_fusion.1
  10.8 0.9 pad_maximum_fusion.3
  11.7 5.0 %collective-permute-start.2 = (bf16[128,8,128]{2,0,1:T(8,128)(2,1)}, bf16[128,8,128]{2,0,1:T(8,128)(2,1)}, u32[]{:S(2)}, u32[]{:S(2)}) collective-permute-start(bf16[128,8,128]{2,0,1:T(8,128)(2,1)} %pad_maximum_fusion.3), channel_id=1, source_target_pairs={{0,3},{4,7},{8,11},{12,15},{16,19},{20,23},{24,27},{28,31}} | collective-permute-start | bytes 786440 | tf_op jit(solution)/shard_map/ppermute | solution.py:16
  16.7 2.0 collective-permute-start
  18.7 2.0 collective-permute-start.1
  20.8 0.8 copy.187
  21.7 2.0 collective-permute-start.3
  23.6 2.0 collective-permute-start.4
  25.9 0.3 multiply_reduce_fusion.2
  26.5 0.3 multiply_multiply_fusion
  26.8 0.5 subtract_convert_fusion
  28.5 1.4 reshape_squeeze.7
  29.9 1.2 copy.224
  31.4 1.5 collective-permute-start.5
  32.9 2.1 fusion.7
  35.0 0.9 fusion.6
  35.9 3.9 %collective-permute-done.5 = bf16[128,8,128]{2,0,1:T(8,128)(2,1)S(1)} collective-permute-done((bf16[128,8,128]{2,0,1:T(8,128)(2,1)}, bf16[128,8,128]{2,0,1:T(8,128)(2,1)S(1)}, u32[]{:S(2)}, u32[]{:S(2)}) %collective-permute-start.5) | collective-permute-done | bytes 262176 | tf_op jit(solution)/shard_map/ppermute | solution.py:16
  39.8 2.4 fusion.2
  42.2 1.3 fusion.4
  43.6 1.7 fusion.21
  45.2 2.2 fusion.57
  47.4 3.0 fusion.56
  50.5 1.4 copy.237
  51.9 1.4 copy.238
  53.3 0.9 slice_bitcast_fusion.7
  54.2 1.3 collective-permute-start.6
  55.5 1.3 collective-permute-start.7
  56.8 1.3 collective-permute-start.8
  58.1 1.8 multiply_add_fusion.1
  59.8 0.9 multiply_reduce_fusion
  60.9 1.8 fusion.22
  62.7 1.3 concatenate.51
  64.0 1.2 slice_bitcast_fusion.4
  65.2 1.3 collective-permute-start.10
  66.5 1.3 collective-permute-start.11
  67.8 1.3 collective-permute-start.9
  69.3 1.7 collective-permute-done.8
  71.0 1.4 fusion.40
  72.4 0.3 multiply_add_fusion.3
  72.7 0.5 multiply_reduce_fusion.3
  73.2 0.5 fusion.33
  74.0 2.3 collective-permute-done.10
  76.3 6.4 %collective-permute-done.11 = bf16[128,8,128]{0,2,1:T(8,128)(2,1)S(1)} collective-permute-done((bf16[128,8,128]{0,2,1:T(8,128)(2,1)S(1)}, bf16[128,8,128]{0,2,1:T(8,128)(2,1)S(1)}, u32[]{:S(2)}, u32[]{:S(2)}) %collective-permute-start.11) | collective-permute-done | bytes 262176 | tf_op jit(solution)/shard_map/ppermute | solution.py:16
  82.7 1.2 fusion.37
  84.0 1.0 pad_maximum_fusion.1
  85.1 0.3 reduce-scatter.2.cloned.1.call-start
  85.4 6.3 %copy.211 = bf16[1,128,5376]{1,0,2:T(2,128)(2,1)S(1)} copy(bf16[1,128,5376]{2,1,0:T(8,128)(2,1)} %param.10) | data formatting | bytes 2752512 | tf_op args[0]
  91.7 0.5 broadcast.142
  92.2 30.3 %reduce = bf16[5376,128]{1,0:T(8,128)(2,1)} reduce(bf16[5376,1,128]{2,1,0:T(2,128)(2,1)S(1)} %bitcast.178, bf16[]{:T(256)} %broadcast.142), dimensions={1}, to_apply=%bitcast.157.reduce_sub_computation | reduce | bytes 2752514
  122.4 3.2 %reshape.256 = bf16[8,2,43008]{2,1,0:T(2,128)(2,1)S(1)} reshape(bf16[5376,128]{1,0:T(8,128)(2,1)} %reduce) | data formatting | bytes 2752512
  125.7 71.0 %all_to_all.36 = bf16[8,2,43008]{2,1,0:T(2,128)(2,1)} all-to-all(bf16[8,2,43008]{2,1,0:T(2,128)(2,1)S(1)} %reshape.256), channel_id=1, replica_groups=mesh['dp'=8,'ctx'=4] {'dp'}, dimensions={0} | all-to-all | bytes 2752512 | tf_op jit(solution)/shard_map/all_to_all | solution.py:50
  196.7 4.5 %reshape.257 = bf16[5376,1,128]{2,1,0:T(2,128)(2,1)S(1)} reshape(bf16[8,2,43008]{2,1,0:T(2,128)(2,1)} %all_to_all.36) | data formatting | bytes 2752512
  201.2 1.3 copy.236
  202.5 29.1 %all-gather.2.cloned.1.call-done = bf16[8,128,4096]{2,1,0:T(8,128)(2,1)} async-done(((bf16[1,128,4096]{2,1,0:T(8,128)(2,1)}), bf16[8,128,4096]{2,1,0:T(8,128)(2,1)}) %all-gather.2.cloned.1.call-update) | async-done | bytes 8388624 | tf_op jit(solution)/shard_map/all_gather | solution.py:120
  231.6 10.2 %bitcast_convert_fusion = bf16[4096,672]{0,1:T(8,128)(2,1)} fusion(bf16[8,128,672]{1,2,0:T(8,128)(2,1)} %bitcast.192, bf16[8,128,4096]{2,1,0:T(8,128)(2,1)} %all-gather.2.cloned.1.call-done), kind=kOutput, calls=%fused_computation | convolution fusion | flops 5639897088 | bytes 15269888 | tf_op jit(solution)/shard_map/btp,btd->pd/dot_general | solution.py:126
  241.8 11.1 %fusion.18 = bf16[8,128,672]{1,2,0:T(8,128)(2,1)} fusion(bf16[8,128,4096]{2,1,0:T(8,128)(2,1)} %all-gather.2.cloned.1.call-done, bf16[672,4096]{1,0:T(8,128)(2,1)} %param.19), kind=kOutput, calls=%fused_computation.20 | convolution fusion | flops 5637832704 | bytes 15269888 | tf_op jit(solution)/shard_map/btp,dp->btd/dot_general | solution.py:121
  252.9 3.6 %all-to-all-start = ((bf16[8,128,672]{1,2,0:T(8,128)(2,1)}), bf16[8,128,672]{1,2,0:T(8,128)(2,1)S(1)}, u32[]{:S(2)}, u32[]{:S(2)}) async-start(bf16[8,128,672]{1,2,0:T(8,128)(2,1)} %fusion.18), calls=%async_computation | async-start | bytes 2752512 | tf_op jit(solution)/shard_map/all_to_all | solution.py:122
  256.4 53.0 %all-reduce.4 = (f32[128]{0:T(128)}, f32[128]{0:T(128)}) all-reduce(f32[128]{0:T(128)S(1)} %get-tuple-element.28, f32[128]{0:T(128)S(1)} %get-tuple-element.30), channel_id=1, replica_groups=mesh['dp'=8,'ctx'=4] {'dp','ctx'}, use_global_device_ids=true, to_apply=%region_9.10 | all-reduce | flops 256 | bytes 2048 | tf_op jit(solution)/shard_map/psum | solution.py:117
  309.5 1.5 copy.212
  311.0 3.2 %convert_element_type.126 = f32[1024,672]{0,1:T(8,128)} convert(bf16[1024,672]{0,1:T(8,128)(2,1)} %reduce-scatter.2.cloned.1.call-done) | non-fusion elementwise | flops 688128 | bytes 4128768 | tf_op jit(solution)/shard_map/convert_element_type | solution.py:132
  (54 shorter events, 2.7 us)
Async XLA Ops:
  7.2 13.5 %copy-start.4 = (bf16[1,128,1024]{2,1,0:T(8,128)(2,1)S(1)}, bf16[1,128,1024]{2,1,0:T(8,128)(2,1)}, u32[]{:S(2)}) copy-start(bf16[1,128,1024]{2,1,0:T(8,128)(2,1)} %param.13) | copy-start | bytes 786436
  7.2 18.5 %copy-start.2 = (bf16[1,128,2048]{2,1,0:T(8,128)(2,1)S(1)}, bf16[1,128,2048]{2,1,0:T(8,128)(2,1)}, u32[]{:S(2)}) copy-start(bf16[1,128,2048]{2,1,0:T(8,128)(2,1)} %param.11) | copy-start | bytes 1572868
  7.2 224.4 %all-gather.2.cloned.1.call-start = ((), (), s32[]{:S(2)}) async-start(), calls=%async_computation.3 | async-start | bytes 9437184 | tf_op jit(solution)/shard_map/all_gather | solution.py:120
  8.6 17.0 %copy-start = (f32[128,8,128]{2,0,1:T(8,128)}, f32[128,8,128]{2,0,1:T(8,128)S(1)}, u32[]{:S(2)}) copy-start(f32[128,8,128]{2,0,1:T(8,128)S(1)} %copy.177) | copy-start | bytes 1572868
  10.5 15.9 %copy-start.5 = (f32[128]{0:T(128)S(1)}, f32[128]{0:T(128)}, u32[]{:S(2)}) copy-start(f32[128]{0:T(128)} %param.17) | copy-start | bytes 1540
  11.7 19.7 %collective-permute-start.2 = (bf16[128,8,128]{2,0,1:T(8,128)(2,1)}, bf16[128,8,128]{2,0,1:T(8,128)(2,1)}, u32[]{:S(2)}, u32[]{:S(2)}) collective-permute-start(bf16[128,8,128]{2,0,1:T(8,128)(2,1)} %pad_maximum_fusion.3), channel_id=1, source_target_pairs={{0,3},{4,7},{8,11},{12,15},{16,19},{20,23},{24,27},{28,31}} | collective-permute-start | bytes 786440 | tf_op jit(solution)/shard_map/ppermute | solution.py:16
  16.7 16.2 %collective-permute-start = (bf16[128,8,128]{2,0,1:T(8,128)(2,1)}, bf16[128,8,128]{2,0,1:T(8,128)(2,1)}, u32[]{:S(2)}, u32[]{:S(2)}) collective-permute-start(bf16[128,8,128]{2,0,1:T(8,128)(2,1)} %pad_maximum_fusion.3), channel_id=1, source_target_pairs={{0,1},{1,2},{2,3},{4,5},{5,6},{6,7},{8,9},{9,10},{10,11},{12,13},{... | collective-permute-start | bytes 786440 | tf_op jit(solution)/shard_map/ppermute | solution.py:16
  18.7 14.3 %collective-permute-start.1 = (bf16[128,8,128]{2,0,1:T(8,128)(2,1)}, bf16[128,8,128]{2,0,1:T(8,128)(2,1)}, u32[]{:S(2)}, u32[]{:S(2)}) collective-permute-start(bf16[128,8,128]{2,0,1:T(8,128)(2,1)} %pad_maximum_fusion.3), channel_id=1, source_target_pairs={{0,2},{1,3},{4,6},{5,7},{8,10},{9,11},{12,14},{13,15},{16,18},{17,... | collective-permute-start | bytes 786440 | tf_op jit(solution)/shard_map/ppermute | solution.py:16
  21.7 14.2 %collective-permute-start.3 = (bf16[128,8,128]{2,0,1:T(8,128)(2,1)}, bf16[128,8,128]{2,0,1:T(8,128)(2,1)}, u32[]{:S(2)}, u32[]{:S(2)}) collective-permute-start(bf16[128,8,128]{2,0,1:T(8,128)(2,1)} %copy.187), channel_id=1, source_target_pairs={{0,1},{1,2},{2,3},{4,5},{5,6},{6,7},{8,9},{9,10},{10,11},{12,13},{... | collective-permute-start | bytes 786440 | tf_op jit(solution)/shard_map/ppermute | solution.py:16
  23.6 12.3 %collective-permute-start.4 = (bf16[128,8,128]{2,0,1:T(8,128)(2,1)}, bf16[128,8,128]{2,0,1:T(8,128)(2,1)}, u32[]{:S(2)}, u32[]{:S(2)}) collective-permute-start(bf16[128,8,128]{2,0,1:T(8,128)(2,1)} %copy.187), channel_id=1, source_target_pairs={{0,2},{1,3},{4,6},{5,7},{8,10},{9,11},{12,14},{13,15},{16,18},{17,... | collective-permute-start | bytes 786440 | tf_op jit(solution)/shard_map/ppermute | solution.py:16
  26.8 4.5 %copy-start.7 = (s32[1,128]{1,0:T(1,128)S(1)}, s32[1,128]{1,0:T(1,128)}, u32[]{:S(2)}) copy-start(s32[1,128]{1,0:T(1,128)} %param.15) | copy-start | bytes 1540
  31.4 8.4 %collective-permute-start.5 = (bf16[128,8,128]{2,0,1:T(8,128)(2,1)}, bf16[128,8,128]{2,0,1:T(8,128)(2,1)S(1)}, u32[]{:S(2)}, u32[]{:S(2)}) collective-permute-start(bf16[128,8,128]{2,0,1:T(8,128)(2,1)} %copy.187), channel_id=1, source_target_pairs={{0,3},{4,7},{8,11},{12,15},{16,19},{20,23},{24,27},{28,31}} | collective-permute-start | bytes 786440 | tf_op jit(solution)/shard_map/ppermute | solution.py:16
  35.0 4.8 %copy-start.3 = (bf16[128,8,2,128,1]{0,3,2,4,1:T(8,128)(2,1)S(1)}, bf16[128,8,2,128,1]{0,3,2,4,1:T(8,128)(2,1)}, u32[]{:S(2)}) copy-start(bf16[128,8,2,128,1]{0,3,2,4,1:T(8,128)(2,1)} %copy.224) | copy-start | bytes 1572868
  54.2 13.7 %collective-permute-start.6 = (bf16[128,8,128]{2,0,1:T(8,128)(2,1)}, bf16[128,8,128]{2,0,1:T(8,128)(2,1)}, u32[]{:S(2)}, u32[]{:S(2)}) collective-permute-start(bf16[128,8,128]{2,0,1:T(8,128)(2,1)} %get-tuple-element.40), channel_id=1, source_target_pairs={{1,0},{2,1},{3,2},{5,4},{6,5},{7,6},{9,8},{10,9},{11,10},{13,12},{... | collective-permute-start | bytes 786440 | tf_op jit(solution)/shard_map/ppermute | solution.py:16
  55.5 13.8 %collective-permute-start.7 = (bf16[128,8,128]{2,0,1:T(8,128)(2,1)}, bf16[128,8,128]{2,0,1:T(8,128)(2,1)}, u32[]{:S(2)}, u32[]{:S(2)}) collective-permute-start(bf16[128,8,128]{2,0,1:T(8,128)(2,1)} %get-tuple-element.42), channel_id=1, source_target_pairs={{2,0},{3,1},{6,4},{7,5},{10,8},{11,9},{14,12},{15,13},{18,16},{19,... | collective-permute-start | bytes 786440 | tf_op jit(solution)/shard_map/ppermute | solution.py:16
  56.8 14.2 %collective-permute-start.8 = (bf16[128,8,128]{2,0,1:T(8,128)(2,1)}, bf16[128,8,128]{2,0,1:T(8,128)(2,1)}, u32[]{:S(2)}, u32[]{:S(2)}) collective-permute-start(bf16[128,8,128]{2,0,1:T(8,128)(2,1)} %get-tuple-element.41), channel_id=1, source_target_pairs={{3,0},{7,4},{11,8},{15,12},{19,16},{23,20},{27,24},{31,28}} | collective-permute-start | bytes 786440 | tf_op jit(solution)/shard_map/ppermute | solution.py:16
  62.7 9.9 %copy-start.1 = (f32[128,8,128]{2,0,1:T(8,128)S(1)}, f32[128,8,128]{2,0,1:T(8,128)}, u32[]{:S(2)}) copy-start(f32[128,8,128]{2,0,1:T(8,128)} %copy-done) | copy-start | bytes 1572868
  62.7 9.9 %copy-start.6 = (f32[128]{0:T(128)S(1)}, f32[128]{0:T(128)}, u32[]{:S(2)}) copy-start(f32[128]{0:T(128)} %param.18) | copy-start | bytes 1540
  65.2 11.1 %collective-permute-start.10 = (bf16[128,8,128]{0,2,1:T(8,128)(2,1)S(1)}, bf16[128,8,128]{0,2,1:T(8,128)(2,1)S(1)}, u32[]{:S(2)}, u32[]{:S(2)}) collective-permute-start(bf16[128,8,128]{0,2,1:T(8,128)(2,1)S(1)} %get-tuple-element.45), channel_id=1, source_target_pairs={{2,0},{3,1},{6,4},{7,5},{10,8},{11,9},{14,12},{15,13},{18,16},{19,... | collective-permute-start | bytes 786440 | tf_op jit(solution)/shard_map/ppermute | solution.py:16
  66.5 16.2 %collective-permute-start.11 = (bf16[128,8,128]{0,2,1:T(8,128)(2,1)S(1)}, bf16[128,8,128]{0,2,1:T(8,128)(2,1)S(1)}, u32[]{:S(2)}, u32[]{:S(2)}) collective-permute-start(bf16[128,8,128]{0,2,1:T(8,128)(2,1)S(1)} %get-tuple-element.44), channel_id=1, source_target_pairs={{3,0},{7,4},{11,8},{15,12},{19,16},{23,20},{27,24},{31,28}} | collective-permute-start | bytes 786440 | tf_op jit(solution)/shard_map/ppermute | solution.py:16
  67.8 14.9 %collective-permute-start.9 = (bf16[128,8,128]{0,2,1:T(8,128)(2,1)S(1)}, bf16[128,8,128]{0,2,1:T(8,128)(2,1)S(1)}, u32[]{:S(2)}, u32[]{:S(2)}) collective-permute-start(bf16[128,8,128]{0,2,1:T(8,128)(2,1)S(1)} %get-tuple-element.43), channel_id=1, source_target_pairs={{1,0},{2,1},{3,2},{5,4},{6,5},{7,6},{9,8},{10,9},{11,10},{13,12},{... | collective-permute-start | bytes 786440 | tf_op jit(solution)/shard_map/ppermute | solution.py:16
  85.1 225.9 %reduce-scatter.2.cloned.1.call-start = ((), (), s32[]{:S(2)}) async-start(), calls=%async_computation.4 | async-start | bytes 6881280 | tf_op jit(solution)/shard_map/reduce_scatter | solution.py:125
  252.9 56.6 %all-to-all-start = ((bf16[8,128,672]{1,2,0:T(8,128)(2,1)}), bf16[8,128,672]{1,2,0:T(8,128)(2,1)S(1)}, u32[]{:S(2)}, u32[]{:S(2)}) async-start(bf16[8,128,672]{1,2,0:T(8,128)(2,1)} %fusion.18), calls=%async_computation | async-start | bytes 2752512 | tf_op jit(solution)/shard_map/all_to_all | solution.py:122
Sparse Core Ops, SparseCore 0:
  85.2 146.3 all-gather.1
  241.9 51.8 reduce-scatter.1
where the time goes:
time: 322 us; the launch traced here: 321 us
  blocking collectives  124 us (39%)
  other arithmetic  49.7 us (15%)
  waiting for transfers between devices  43.6 us (14%)
  matrix products  32.5 us (10%)
  local copies, waits for them, and re-layouts  30 us (9%)
  starting transfers between devices  26 us (8%)
  between operations  15.2 us (5%)
    all_to_all x1, blocking collectives, shards(): lax.all_to_all(inputs, 'dp', split_axis=2, concat_axis=0, tiled=True)  71 us
    psum x1, blocking collectives, shards(): dq_gain_all, dk_gain_all = lax.psum((dq_gain, dk_gain), ('dp', 'ctx'))  53 us
    unnamed x2, other arithmetic  30.4 us
    all_gather x1, waiting for transfers between devices, shards(): gathered = lax.all_gather(d_proj, 'dp', axis=0, tiled=True)  29.1 us
    ppermute x12, starting transfers between devices, from_behind(): lax.ppermute(value, axis, [(source, source + steps) for source in range(i...  22.2 us
    unnamed x27, local copies, waits for them, and re-layouts  21.7 us
    ppermute x12, waiting for transfers between devices, from_behind(): lax.ppermute(value, axis, [(source, source + steps) for source in range(i...  14.4 us
    dot_general x1, matrix products, shards(): jnp.einsum('btp,dp->btd', gathered, weight, preferred_element_type=jnp.fl...  11.1 us
  transfers between devices with their start and end apart: 15, of which 6 were waited for; matrix products, arithmetic and copies ran while one was open for 24% of the time, Pallas kernels for 0%

commit v1 on v0

--- a/solution.py
+++ b/solution.py
@@ -8,6 +8,14 @@
 score_scale = 168.0 ** (-0.5)
 rope_base = 10000.0
 norm_eps = 1e-06
+
+
+def pairs_all_keep_up(block_in, join_dim):
+    block_in = jnp.moveaxis(block_in, 0, join_dim)
+    side_arr = block_in.shape
+    return block_in.reshape(
+        *side_arr[:join_dim], side_arr[join_dim] * side_arr[join_dim + 1], *side_arr[join_dim + 2 :]
+    )
 
 
 def from_behind(value, axis, steps):
@@ -117,7 +125,18 @@
     dq_gain_all, dk_gain_all = lax.psum((dq_gain, dk_gain), ("dp", "ctx"))
     dv_proj = dv_total.reshape(tok_rows, key_heads * head_width)
     d_proj = jnp.concatenate([dq_proj, dk_proj, dv_proj], axis=-1).astype(jnp.bfloat16)[None]
-    gathered = lax.all_gather(d_proj, "dp", axis=0, tiled=True)
+    n_parts = jax.lax.axis_size("dp")
+    copies = []
+    for m in range(n_parts):
+        copies.append((m, (m + 1) % n_parts))
+    seen = [d_proj]
+    while len(seen) < n_parts:
+        t_next = jax.lax.ppermute(seen[-1], "dp", copies)
+        seen.append(t_next)
+    oldest = jax.lax.axis_index("dp")
+    carry_out = jnp.stack(seen, axis=0)
+    seen = carry_out[(oldest - jnp.arange(n_parts)) % n_parts]
+    gathered = pairs_all_keep_up(seen, 0)
     d_cols = jnp.einsum("btp,dp->btd", gathered, weight, preferred_element_type=jnp.float32)
     d_inputs = lax.all_to_all(
         d_cols.astype(jnp.bfloat16), "dp", split_axis=0, concat_axis=2, tiled=True

time: 322 us -> 418 us (1.30)
  waiting for transfers between devices: 43.6 us -> 154 us
  blocking collectives: 124 us -> 45.8 us
  starting transfers between devices: 26 us -> 75 us
  local copies, waits for them, and re-layouts: 30 us -> 47.2 us
    ppermute x0 -> x7, waiting for transfers between devices: none -> 136 us  [shards(): t_next = jax.lax.ppermute(seen[-1], 'dp', copies)]
    all_to_all x1 -> x0, blocking collectives: 71 us -> none  [shards(): lax.all_to_all(inputs, 'dp', split_axis=2, concat_axis=0, tiled=True)]
    ppermute x0 -> x7, starting transfers between devices: none -> 43 us  [shards(): t_next = jax.lax.ppermute(seen[-1], 'dp', copies)]
    all_gather x1 -> x0, waiting for transfers between devices: 29.1 us -> none  [shards(): gathered = lax.all_gather(d_proj, 'dp', axis=0, tiled=True)]
    unnamed x27 -> x58, local copies, waits for them, and re-layouts: 21.7 us -> 31.3 us
    gather x0 -> x1, local copies, waits for them, and re-layouts: none -> 8.16 us  [shards(): seen = carry_out[(oldest - jnp.arange(n_parts)) % n_parts]]
    psum x1, blocking collectives: 53 us -> 45.8 us  [shards(): dq_gain_all, dk_gain_all = lax.psum((dq_gain, dk_gain), ('dp', 'ctx'))]
    all_to_all x0 -> x1, starting transfers between devices: none -> 5.99 us  [shards(): lax.all_to_all(inputs, 'dp', split_axis=2, concat_axis=0, tiled=True)]
  transfers between devices with their start and end apart: 15 -> 22, of which waited for: 6 -> 10; matrix products, arithmetic and copies ran while one was open for 24% -> 21% of each run, Pallas kernels for 0% -> 0%
where the time goes in v1:
time: 418 us; the launch traced here: 417 us
  waiting for transfers between devices  154 us (37%)
  starting transfers between devices  75 us (18%)
  local copies, waits for them, and re-layouts  47.2 us (11%)
  other arithmetic  46.5 us (11%)
  blocking collectives  45.8 us (11%)
  matrix products  32.9 us (8%)
  between operations  15.3 us (4%)
    ppermute x7, waiting for transfers between devices, shards(): t_next = jax.lax.ppermute(seen[-1], 'dp', copies)  136 us
    psum x1, blocking collectives, shards(): dq_gain_all, dk_gain_all = lax.psum((dq_gain, dk_gain), ('dp', 'ctx'))  45.8 us
    ppermute x7, starting transfers between devices, shards(): t_next = jax.lax.ppermute(seen[-1], 'dp', copies)  43 us
    unnamed x58, local copies, waits for them, and re-layouts  31.3 us
    unnamed x2, other arithmetic  31.3 us
    ppermute x12, starting transfers between devices, from_behind(): lax.ppermute(value, axis, [(source, source + steps) for source in range(i...  22.3 us
    ppermute x12, waiting for transfers between devices, from_behind(): lax.ppermute(value, axis, [(source, source + steps) for source in range(i...  17.7 us
    dot_general x1, matrix products, shards(): jnp.einsum('btp,dp->btd', gathered, weight, preferred_element_type=jnp.fl...  12.1 us
  transfers between devices with their start and end apart: 22, of which 10 were waited for; matrix products, arithmetic and copies ran while one was open for 21% of the time, Pallas kernels for 0%

profile of v1, /device:TPU:0, one launch (start us, length us, event | category | flops | bytes accessed | tf_op | source)
XLA Modules:
  0.0 416.6 jit_solution(13690136980927753644)
XLA Ops:
  7.2 1.2 copy.144
  10.1 0.9 multiply_multiply_fusion.1
  11.2 0.9 pad_maximum_fusion.3
  12.1 5.0 %collective-permute-start.2 = (bf16[128,8,128]{2,0,1:T(8,128)(2,1)}, bf16[128,8,128]{2,0,1:T(8,128)(2,1)}, u32[]{:S(2)}, u32[]{:S(2)}) collective-permute-start(bf16[128,8,128]{2,0,1:T(8,128)(2,1)} %pad_maximum_fusion.3), channel_id=1, source_target_pairs={{0,3},{4,7},{8,11},{12,15},{16,19},{20,23},{24,27},{28,31}} | collective-permute-start | bytes 786440 | tf_op jit(solution)/shard_map/ppermute | solution.py:24
  17.1 2.0 collective-permute-start
  19.1 2.0 collective-permute-start.1
  21.2 0.9 copy.156
  22.1 2.0 collective-permute-start.3
  24.1 2.0 collective-permute-start.4
  27.5 0.9 maximum_bitcast_fusion.2
  29.6 1.4 reshape_squeeze.7
  31.0 1.2 copy.190
  32.2 0.8 copy.159
  33.8 1.3 collective-permute-start.5
  35.2 2.1 fusion.7
  37.3 0.9 fusion.6
  38.2 2.0 collective-permute-done.5
  40.3 2.4 fusion.2
  42.7 1.3 fusion.4
  44.1 1.7 fusion.21
  46.6 2.6 fusion.57
  49.4 0.9 multiply_reduce_fusion
  50.4 1.3 collective-permute-start.6
  51.7 1.3 collective-permute-start.7
  53.0 1.3 collective-permute-start.8
  54.3 0.9 slice_bitcast_fusion.4
  55.2 1.4 collective-permute-start.10
  56.6 1.5 collective-permute-start.11
  58.4 1.3 collective-permute-start.9
  59.7 2.9 collective-permute-done.7
  62.6 5.9 %collective-permute-done.8 = bf16[128,8,128]{2,0,1:T(8,128)(2,1)S(1)} collective-permute-done((bf16[128,8,128]{2,0,1:T(8,128)(2,1)S(1)}, bf16[128,8,128]{2,0,1:T(8,128)(2,1)S(1)}, u32[]{:S(2)}, u32[]{:S(2)}) %collective-permute-start.8) | collective-permute-done | bytes 262176 | tf_op jit(solution)/shard_map/ppermute | solution.py:24
  70.2 6.8 %collective-permute-done.11 = bf16[128,8,128]{0,2,1:T(8,128)(2,1)} collective-permute-done((bf16[128,8,128]{0,2,1:T(8,128)(2,1)}, bf16[128,8,128]{0,2,1:T(8,128)(2,1)}, u32[]{:S(2)}, u32[]{:S(2)}) %collective-permute-start.11) | collective-permute-done | bytes 262176 | tf_op jit(solution)/shard_map/ppermute | solution.py:24
  76.9 1.3 fusion.37
  78.3 1.5 collective-permute-start.12
  79.9 23.4 %collective-permute-done.12 = bf16[1,128,4096]{1,2,0:T(8,128)(2,1)S(1)} collective-permute-done((bf16[1,128,4096]{1,2,0:T(8,128)(2,1)S(1)}, bf16[1,128,4096]{1,2,0:T(8,128)(2,1)S(1)}, u32[]{:S(2)}, u32[]{:S(2)}) %collective-permute-start.12) | collective-permute-done | bytes 1048608 | tf_op jit(solution)/shard_map/ppermute | solution.py:134
  103.3 24.1 %collective-permute-done.13 = bf16[1,128,4096]{1,2,0:T(8,128)(2,1)} collective-permute-done((bf16[1,128,4096]{1,2,0:T(8,128)(2,1)S(1)}, bf16[1,128,4096]{1,2,0:T(8,128)(2,1)}, u32[]{:S(2)}, u32[]{:S(2)}) %collective-permute-start.13) | collective-permute-done | bytes 1048608 | tf_op jit(solution)/shard_map/ppermute | solution.py:134
  127.3 6.3 %copy.176 = bf16[1,128,5376]{1,0,2:T(2,128)(2,1)S(1)} copy(bf16[1,128,5376]{2,1,0:T(8,128)(2,1)} %param.10) | data formatting | bytes 2752512 | tf_op args[0]
  134.1 30.3 %reduce = bf16[5376,128]{1,0:T(8,128)(2,1)} reduce(bf16[5376,1,128]{2,1,0:T(2,128)(2,1)S(1)} %bitcast.195, bf16[]{:T(256)} %broadcast.211), dimensions={1}, to_apply=%bitcast.172.reduce_sub_computation | reduce | bytes 2752514
  164.4 4.2 %reshape.368 = bf16[8,2,43008]{2,1,0:T(2,128)(2,1)} reshape(bf16[5376,128]{1,0:T(8,128)(2,1)} %reduce) | data formatting | bytes 2752512
  168.6 6.0 %all-to-all-start.1 = ((bf16[8,2,43008]{2,1,0:T(2,128)(2,1)}), bf16[8,2,43008]{2,1,0:T(2,128)(2,1)}, u32[]{:S(2)}, u32[]{:S(2)}) async-start(bf16[8,2,43008]{2,1,0:T(2,128)(2,1)} %reshape.368), calls=%async_computation.1 | async-start | bytes 2752512 | tf_op jit(solution)/shard_map/all_to_all | solution.py:58
  174.7 2.0 collective-permute-start.15
  176.7 1.1 maximum_dynamic-update-slice_fusion
  177.8 42.3 %collective-permute-done.15 = bf16[1,128,4096]{1,2,0:T(8,128)(2,1)} collective-permute-done((bf16[1,128,4096]{1,2,0:T(8,128)(2,1)}, bf16[1,128,4096]{1,2,0:T(8,128)(2,1)}, u32[]{:S(2)}, u32[]{:S(2)}) %collective-permute-start.15) | collective-permute-done | bytes 1048608 | tf_op jit(solution)/shard_map/ppermute | solution.py:134
  220.1 1.0 bitcast_dynamic-update-slice_fusion.6
  221.1 4.5 %reshape.369 = bf16[5376,1,128]{2,1,0:T(2,128)(2,1)S(1)} reshape(bf16[8,2,43008]{2,1,0:T(2,128)(2,1)} %all-to-all-done.1) | data formatting | bytes 2752512
  225.7 1.3 copy.204
  227.0 2.3 bitcast_dynamic-update-slice_fusion.5
  229.2 13.3 %collective-permute-done.16 = bf16[1,128,4096]{1,2,0:T(8,128)(2,1)} collective-permute-done((bf16[1,128,4096]{1,2,0:T(8,128)(2,1)}, bf16[1,128,4096]{1,2,0:T(8,128)(2,1)}, u32[]{:S(2)}, u32[]{:S(2)}) %collective-permute-start.16) | collective-permute-done | bytes 1048608 | tf_op jit(solution)/shard_map/ppermute | solution.py:134
  242.5 37.1 %collective-permute-start.17 = (bf16[1,128,4096]{1,2,0:T(8,128)(2,1)}, bf16[1,128,4096]{1,2,0:T(8,128)(2,1)S(1)}, u32[]{:S(2)}, u32[]{:S(2)}) collective-permute-start(bf16[1,128,4096]{1,2,0:T(8,128)(2,1)} %collective-permute-done.16), channel_id=1, source_target_pairs={{0,4},{4,8},{8,12},{12,16},{16,20},{20,24},{24,28},{28,0},{1,5},{5... | collective-permute-start | bytes 3145736 | tf_op jit(solution)/shard_map/ppermute | solution.py:134
  279.6 2.3 bitcast_dynamic-update-slice_fusion.4
  281.8 2.3 bitcast_dynamic-update-slice_fusion.3
  284.1 16.6 %collective-permute-done.17 = bf16[1,128,4096]{1,2,0:T(8,128)(2,1)S(1)} collective-permute-done((bf16[1,128,4096]{1,2,0:T(8,128)(2,1)}, bf16[1,128,4096]{1,2,0:T(8,128)(2,1)S(1)}, u32[]{:S(2)}, u32[]{:S(2)}) %collective-permute-start.17) | collective-permute-done | bytes 1048608 | tf_op jit(solution)/shard_map/ppermute | solution.py:134
  300.7 2.4 collective-permute-start.18
  303.1 2.3 bitcast_dynamic-update-slice_fusion.2
  305.4 1.0 bitcast_dynamic-update-slice_fusion.1
  306.4 16.6 %collective-permute-done.18 = bf16[1,128,4096]{1,2,0:T(8,128)(2,1)S(1)} collective-permute-done((bf16[1,128,4096]{1,2,0:T(8,128)(2,1)S(1)}, bf16[1,128,4096]{1,2,0:T(8,128)(2,1)S(1)}, u32[]{:S(2)}, u32[]{:S(2)}) %collective-permute-start.18) | collective-permute-done | bytes 1048608 | tf_op jit(solution)/shard_map/ppermute | solution.py:134
  323.0 1.1 bitcast_dynamic-update-slice_fusion
  324.2 8.2 %gather_fusion = bf16[8,128,4096]{1,2,0:T(8,128)(2,1)} fusion(bf16[8,128,4096]{1,2,0:T(8,128)(2,1)} %bitcast.64, s32[1024]{0:T(1024)S(1)} %pad_clamp_fusion), kind=kCustom, calls=%fused_computation | custom fusion | bytes 16777248 | tf_op jit(solution)/shard_map/gather | solution.py:138
  332.4 11.2 %bitcast_convert_fusion = bf16[4096,672]{0,1:T(8,128)(2,1)} fusion(bf16[8,128,4096]{1,2,0:T(8,128)(2,1)} %gather_fusion, bf16[8,128,672]{1,2,0:T(8,128)(2,1)S(1)} %bitcast.215), kind=kOutput, calls=%fused_computation.1 | convolution fusion | flops 5639897088 | bytes 15269888 | tf_op jit(solution)/shard_map/btp,btd->pd/dot_general | solution.py:145
  343.5 12.1 %fusion.18 = bf16[8,128,672]{1,2,0:T(8,128)(2,1)} fusion(bf16[8,128,4096]{1,2,0:T(8,128)(2,1)} %gather_fusion, bf16[672,4096]{1,0:T(8,128)(2,1)} %param.19), kind=kOutput, calls=%fused_computation.21 | convolution fusion | flops 5637832704 | bytes 15269888 | tf_op jit(solution)/shard_map/btp,dp->btd/dot_general | solution.py:140
  355.6 3.6 all-to-all-start
  359.2 45.8 %all-reduce.4 = (f32[128]{0:T(128)}, f32[128]{0:T(128)}) all-reduce(f32[128]{0:T(128)S(1)} %copy-done.21, f32[128]{0:T(128)S(1)} %get-tuple-element.26), channel_id=1, replica_groups=mesh['dp'=8,'ctx'=4] {'dp','ctx'}, use_global_device_ids=true, to_apply=%region_9.10 | all-reduce | flops 256 | bytes 2048 | tf_op jit(solution)/shard_map/psum | solution.py:125
  405.1 1.5 copy.178
  406.6 3.2 convert_element_type.133
  (96 shorter events, 8.4 us)
Async XLA Ops:
  7.2 13.9 %copy-start.12 = (bf16[1,128,1024]{2,1,0:T(8,128)(2,1)S(1)}, bf16[1,128,1024]{2,1,0:T(8,128)(2,1)}, u32[]{:S(2)}) copy-start(bf16[1,128,1024]{2,1,0:T(8,128)(2,1)} %param.13) | copy-start | bytes 786436
  7.2 18.9 %copy-start.9 = (bf16[1,128,2048]{2,1,0:T(8,128)(2,1)S(1)}, bf16[1,128,2048]{2,1,0:T(8,128)(2,1)}, u32[]{:S(2)}) copy-start(bf16[1,128,2048]{2,1,0:T(8,128)(2,1)} %param.11) | copy-start | bytes 1572868
  8.4 0.6 copy-start.16
  8.5 18.0 %copy-start.19 = (f32[128]{0:T(128)S(1)}, f32[128]{0:T(128)}, u32[]{:S(2)}) copy-start(f32[128]{0:T(128)} %param.17) | copy-start | bytes 1540
  9.0 17.6 %copy-start.14 = (f32[128,8]{0,1:T(8,128)}, f32[128,8]{0,1:T(8,128)S(1)}, u32[]{:S(2)}) copy-start(f32[128,8]{0,1:T(8,128)S(1)} %fusion.49) | copy-start | bytes 12292
  9.9 16.8 %copy-start.5 = (f32[128,64]{0,1:T(8,128)}, f32[128,64]{0,1:T(8,128)S(1)}, u32[]{:S(2)}) copy-start(f32[128,64]{0,1:T(8,128)S(1)} %get-tuple-element.44) | copy-start | bytes 98308
  9.9 16.8 %copy-start.7 = (f32[128,64]{0,1:T(8,128)}, f32[128,64]{0,1:T(8,128)S(1)}, u32[]{:S(2)}) copy-start(f32[128,64]{0,1:T(8,128)S(1)} %get-tuple-element.45) | copy-start | bytes 98308
  12.1 21.7 %collective-permute-start.2 = (bf16[128,8,128]{2,0,1:T(8,128)(2,1)}, bf16[128,8,128]{2,0,1:T(8,128)(2,1)}, u32[]{:S(2)}, u32[]{:S(2)}) collective-permute-start(bf16[128,8,128]{2,0,1:T(8,128)(2,1)} %pad_maximum_fusion.3), channel_id=1, source_target_pairs={{0,3},{4,7},{8,11},{12,15},{16,19},{20,23},{24,27},{28,31}} | collective-permute-start | bytes 786440 | tf_op jit(solution)/shard_map/ppermute | solution.py:24
  17.1 18.0 %collective-permute-start = (bf16[128,8,128]{2,0,1:T(8,128)(2,1)}, bf16[128,8,128]{2,0,1:T(8,128)(2,1)}, u32[]{:S(2)}, u32[]{:S(2)}) collective-permute-start(bf16[128,8,128]{2,0,1:T(8,128)(2,1)} %pad_maximum_fusion.3), channel_id=1, source_target_pairs={{0,1},{1,2},{2,3},{4,5},{5,6},{6,7},{8,9},{9,10},{10,11},{12,13},{... | collective-permute-start | bytes 786440 | tf_op jit(solution)/shard_map/ppermute | solution.py:24
  19.1 16.1 %collective-permute-start.1 = (bf16[128,8,128]{2,0,1:T(8,128)(2,1)}, bf16[128,8,128]{2,0,1:T(8,128)(2,1)}, u32[]{:S(2)}, u32[]{:S(2)}) collective-permute-start(bf16[128,8,128]{2,0,1:T(8,128)(2,1)} %pad_maximum_fusion.3), channel_id=1, source_target_pairs={{0,2},{1,3},{4,6},{5,7},{8,10},{9,11},{12,14},{13,15},{16,18},{17,... | collective-permute-start | bytes 786440 | tf_op jit(solution)/shard_map/ppermute | solution.py:24
  22.1 16.1 %collective-permute-start.3 = (bf16[128,8,128]{2,0,1:T(8,128)(2,1)}, bf16[128,8,128]{2,0,1:T(8,128)(2,1)}, u32[]{:S(2)}, u32[]{:S(2)}) collective-permute-start(bf16[128,8,128]{2,0,1:T(8,128)(2,1)} %copy.156), channel_id=1, source_target_pairs={{0,1},{1,2},{2,3},{4,5},{5,6},{6,7},{8,9},{9,10},{10,11},{12,13},{... | collective-permute-start | bytes 786440 | tf_op jit(solution)/shard_map/ppermute | solution.py:24
  24.1 14.1 %collective-permute-start.4 = (bf16[128,8,128]{2,0,1:T(8,128)(2,1)}, bf16[128,8,128]{2,0,1:T(8,128)(2,1)}, u32[]{:S(2)}, u32[]{:S(2)}) collective-permute-start(bf16[128,8,128]{2,0,1:T(8,128)(2,1)} %copy.156), channel_id=1, source_target_pairs={{0,2},{1,3},{4,6},{5,7},{8,10},{9,11},{12,14},{13,15},{16,18},{17,... | collective-permute-start | bytes 786440 | tf_op jit(solution)/shard_map/ppermute | solution.py:24
  33.8 6.4 %collective-permute-start.5 = (bf16[128,8,128]{2,0,1:T(8,128)(2,1)}, bf16[128,8,128]{2,0,1:T(8,128)(2,1)S(1)}, u32[]{:S(2)}, u32[]{:S(2)}) collective-permute-start(bf16[128,8,128]{2,0,1:T(8,128)(2,1)} %copy.156), channel_id=1, source_target_pairs={{0,3},{4,7},{8,11},{12,15},{16,19},{20,23},{24,27},{28,31}} | collective-permute-start | bytes 786440 | tf_op jit(solution)/shard_map/ppermute | solution.py:24
  37.3 3.0 copy-start.10
  37.3 3.0 copy-start.13
  42.7 1.4 copy-start.11
  46.6 2.7 copy-start.6
  46.6 2.7 copy-start.8
  46.6 2.8 copy-start.20
  50.4 18.5 %copy-start.15 = (f32[128,8]{0,1:T(8,128)S(1)}, f32[128,8]{0,1:T(8,128)}, u32[]{:S(2)}) copy-start(f32[128,8]{0,1:T(8,128)} %copy-done.14) | copy-start | bytes 12292
  50.4 18.5 %copy-start.18 = (f32[128]{0:T(128)S(1)}, f32[128]{0:T(128)}, u32[]{:S(2)}) copy-start(f32[128]{0:T(128)} %param.18) | copy-start | bytes 1540
  50.4 8.0 %collective-permute-start.6 = (bf16[128,8,128]{2,0,1:T(8,128)(2,1)S(1)}, bf16[128,8,128]{2,0,1:T(8,128)(2,1)S(1)}, u32[]{:S(2)}, u32[]{:S(2)}) collective-permute-start(bf16[128,8,128]{2,0,1:T(8,128)(2,1)S(1)} %get-tuple-element.34), channel_id=1, source_target_pairs={{1,0},{2,1},{3,2},{5,4},{6,5},{7,6},{9,8},{10,9},{11,10},{13,12},{... | collective-permute-start | bytes 786440 | tf_op jit(solution)/shard_map/ppermute | solution.py:24
  51.7 10.9 %collective-permute-start.7 = (bf16[128,8,128]{2,0,1:T(8,128)(2,1)S(1)}, bf16[128,8,128]{2,0,1:T(8,128)(2,1)S(1)}, u32[]{:S(2)}, u32[]{:S(2)}) collective-permute-start(bf16[128,8,128]{2,0,1:T(8,128)(2,1)S(1)} %get-tuple-element.36), channel_id=1, source_target_pairs={{2,0},{3,1},{6,4},{7,5},{10,8},{11,9},{14,12},{15,13},{18,16},{19,... | collective-permute-start | bytes 786440 | tf_op jit(solution)/shard_map/ppermute | solution.py:24
  53.0 15.5 %collective-permute-start.8 = (bf16[128,8,128]{2,0,1:T(8,128)(2,1)S(1)}, bf16[128,8,128]{2,0,1:T(8,128)(2,1)S(1)}, u32[]{:S(2)}, u32[]{:S(2)}) collective-permute-start(bf16[128,8,128]{2,0,1:T(8,128)(2,1)S(1)} %get-tuple-element.35), channel_id=1, source_target_pairs={{3,0},{7,4},{11,8},{15,12},{19,16},{23,20},{27,24},{31,28}} | collective-permute-start | bytes 786440 | tf_op jit(solution)/shard_map/ppermute | solution.py:24
  55.2 14.3 %copy-start.17 = (f32[128,8]{0,1:T(8,128)S(1)}, f32[128,8]{0,1:T(8,128)}, u32[]{:S(2)}) copy-start(f32[128,8]{0,1:T(8,128)} %copy-done.16) | copy-start | bytes 12292
  55.2 15.0 %collective-permute-start.10 = (bf16[128,8,128]{0,2,1:T(8,128)(2,1)}, bf16[128,8,128]{0,2,1:T(8,128)(2,1)}, u32[]{:S(2)}, u32[]{:S(2)}) collective-permute-start(bf16[128,8,128]{0,2,1:T(8,128)(2,1)} %get-tuple-element.39), channel_id=1, source_target_pairs={{2,0},{3,1},{6,4},{7,5},{10,8},{11,9},{14,12},{15,13},{18,16},{19,... | collective-permute-start | bytes 786440 | tf_op jit(solution)/shard_map/ppermute | solution.py:24
  56.6 20.3 %collective-permute-start.11 = (bf16[128,8,128]{0,2,1:T(8,128)(2,1)}, bf16[128,8,128]{0,2,1:T(8,128)(2,1)}, u32[]{:S(2)}, u32[]{:S(2)}) collective-permute-start(bf16[128,8,128]{0,2,1:T(8,128)(2,1)} %get-tuple-element.38), channel_id=1, source_target_pairs={{3,0},{7,4},{11,8},{15,12},{19,16},{23,20},{27,24},{31,28}} | collective-permute-start | bytes 786440 | tf_op jit(solution)/shard_map/ppermute | solution.py:24
  58.4 18.5 %collective-permute-start.9 = (bf16[128,8,128]{0,2,1:T(8,128)(2,1)}, bf16[128,8,128]{0,2,1:T(8,128)(2,1)S(1)}, u32[]{:S(2)}, u32[]{:S(2)}) collective-permute-start(bf16[128,8,128]{0,2,1:T(8,128)(2,1)} %get-tuple-element.37), channel_id=1, source_target_pairs={{1,0},{2,1},{3,2},{5,4},{6,5},{7,6},{9,8},{10,9},{11,10},{13,12},{... | collective-permute-start | bytes 786440 | tf_op jit(solution)/shard_map/ppermute | solution.py:24
  78.2 49.1 %copy-start = (bf16[128,8,128]{0,2,1:T(8,128)(2,1)}, bf16[128,8,128]{0,2,1:T(8,128)(2,1)S(1)}, u32[]{:S(2)}) copy-start(bf16[128,8,128]{0,2,1:T(8,128)(2,1)S(1)} %fusion.37) | copy-start | bytes 786436
  78.3 24.9 %collective-permute-start.12 = (bf16[1,128,4096]{1,2,0:T(8,128)(2,1)S(1)}, bf16[1,128,4096]{1,2,0:T(8,128)(2,1)S(1)}, u32[]{:S(2)}, u32[]{:S(2)}) collective-permute-start(bf16[1,128,4096]{1,2,0:T(8,128)(2,1)S(1)} %pad_maximum_fusion.1), channel_id=1, source_target_pairs={{0,4},{4,8},{8,12},{12,16},{16,20},{20,24},{24,28},{28,0},{1,5},{5... | collective-permute-start | bytes 3145736 | tf_op jit(solution)/shard_map/ppermute | solution.py:134
  103.3 24.1 %copy-start.3 = (bf16[1,128,4096]{1,2,0:T(8,128)(2,1)}, bf16[1,128,4096]{1,2,0:T(8,128)(2,1)S(1)}, u32[]{:S(2)}) copy-start(bf16[1,128,4096]{1,2,0:T(8,128)(2,1)S(1)} %collective-permute-done.12) | copy-start | bytes 3145732
  103.3 24.1 %collective-permute-start.13 = (bf16[1,128,4096]{1,2,0:T(8,128)(2,1)S(1)}, bf16[1,128,4096]{1,2,0:T(8,128)(2,1)}, u32[]{:S(2)}, u32[]{:S(2)}) collective-permute-start(bf16[1,128,4096]{1,2,0:T(8,128)(2,1)S(1)} %collective-permute-done.12), channel_id=1, source_target_pairs={{0,4},{4,8},{8,12},{12,16},{16,20},{20,24},{24,28},{28,0},{1,5},{5... | collective-permute-start | bytes 3145736 | tf_op jit(solution)/shard_map/ppermute | solution.py:134
  127.3 47.3 %collective-permute-start.14 = (bf16[1,128,4096]{1,2,0:T(8,128)(2,1)}, bf16[1,128,4096]{1,2,0:T(8,128)(2,1)}, u32[]{:S(2)}, u32[]{:S(2)}) collective-permute-start(bf16[1,128,4096]{1,2,0:T(8,128)(2,1)} %collective-permute-done.13), channel_id=1, source_target_pairs={{0,4},{4,8},{8,12},{12,16},{16,20},{20,24},{24,28},{28,0},{1,5},{5... | collective-permute-start | bytes 3145736 | tf_op jit(solution)/shard_map/ppermute | solution.py:134
  164.4 12.3 %copy-start.1 = (bf16[128,8,128]{0,2,1:T(8,128)(2,1)S(1)}, bf16[128,8,128]{0,2,1:T(8,128)(2,1)}, u32[]{:S(2)}) copy-start(bf16[128,8,128]{0,2,1:T(8,128)(2,1)} %copy-done) | copy-start | bytes 786436
  164.4 55.7 %copy-start.4 = (bf16[1,128,4096]{1,2,0:T(8,128)(2,1)S(1)}, bf16[1,128,4096]{1,2,0:T(8,128)(2,1)}, u32[]{:S(2)}) copy-start(bf16[1,128,4096]{1,2,0:T(8,128)(2,1)} %copy-done.3) | copy-start | bytes 3145732
  168.6 52.5 %all-to-all-start.1 = ((bf16[8,2,43008]{2,1,0:T(2,128)(2,1)}), bf16[8,2,43008]{2,1,0:T(2,128)(2,1)}, u32[]{:S(2)}, u32[]{:S(2)}) async-start(bf16[8,2,43008]{2,1,0:T(2,128)(2,1)} %reshape.368), calls=%async_computation.1 | async-start | bytes 2752512 | tf_op jit(solution)/shard_map/all_to_all | solution.py:58
  174.6 232.0 %reduce-scatter.2.cloned.1.call-start = ((), (), s32[]{:S(2)}) async-start(), calls=%async_computation.3 | async-start | bytes 6881280 | tf_op jit(solution)/shard_map/reduce_scatter | solution.py:144
  174.7 45.4 %collective-permute-start.15 = (bf16[1,128,4096]{1,2,0:T(8,128)(2,1)}, bf16[1,128,4096]{1,2,0:T(8,128)(2,1)}, u32[]{:S(2)}, u32[]{:S(2)}) collective-permute-start(bf16[1,128,4096]{1,2,0:T(8,128)(2,1)} %collective-permute-done.14), channel_id=1, source_target_pairs={{0,4},{4,8},{8,12},{12,16},{16,20},{20,24},{24,28},{28,0},{1,5},{5... | collective-permute-start | bytes 3145736 | tf_op jit(solution)/shard_map/ppermute | solution.py:134
  220.1 22.4 %collective-permute-start.16 = (bf16[1,128,4096]{1,2,0:T(8,128)(2,1)}, bf16[1,128,4096]{1,2,0:T(8,128)(2,1)}, u32[]{:S(2)}, u32[]{:S(2)}) collective-permute-start(bf16[1,128,4096]{1,2,0:T(8,128)(2,1)} %collective-permute-done.15), channel_id=1, source_target_pairs={{0,4},{4,8},{8,12},{12,16},{16,20},{20,24},{24,28},{28,0},{1,5},{5... | collective-permute-start | bytes 3145736 | tf_op jit(solution)/shard_map/ppermute | solution.py:134
  242.5 58.3 %collective-permute-start.17 = (bf16[1,128,4096]{1,2,0:T(8,128)(2,1)}, bf16[1,128,4096]{1,2,0:T(8,128)(2,1)S(1)}, u32[]{:S(2)}, u32[]{:S(2)}) collective-permute-start(bf16[1,128,4096]{1,2,0:T(8,128)(2,1)} %collective-permute-done.16), channel_id=1, source_target_pairs={{0,4},{4,8},{8,12},{12,16},{16,20},{20,24},{24,28},{28,0},{1,5},{5... | collective-permute-start | bytes 3145736 | tf_op jit(solution)/shard_map/ppermute | solution.py:134
  300.7 22.3 %collective-permute-start.18 = (bf16[1,128,4096]{1,2,0:T(8,128)(2,1)S(1)}, bf16[1,128,4096]{1,2,0:T(8,128)(2,1)S(1)}, u32[]{:S(2)}, u32[]{:S(2)}) collective-permute-start(bf16[1,128,4096]{1,2,0:T(8,128)(2,1)S(1)} %collective-permute-done.17), channel_id=1, source_target_pairs={{0,4},{4,8},{8,12},{12,16},{16,20},{20,24},{24,28},{28,0},{1,5},{5... | collective-permute-start | bytes 3145736 | tf_op jit(solution)/shard_map/ppermute | solution.py:134
  324.2 8.2 %copy-start.2 = (bf16[1,128,5376]{1,2,0:T(8,128)(2,1)S(1)}, bf16[1,128,5376]{1,2,0:T(8,128)(2,1)}, u32[]{:S(2)}) copy-start(bf16[1,128,5376]{1,2,0:T(8,128)(2,1)} %copy.204) | copy-start | bytes 4128772
  343.5 15.7 %copy-start.21 = (f32[128]{0:T(128)S(1)}, f32[128]{0:T(128)}, u32[]{:S(2)}) copy-start(f32[128]{0:T(128)} %get-tuple-element.24) | copy-start | bytes 1540
  355.6 49.4 %all-to-all-start = ((bf16[8,128,672]{1,2,0:T(8,128)(2,1)}), bf16[8,128,672]{1,2,0:T(8,128)(2,1)S(1)}, u32[]{:S(2)}, u32[]{:S(2)}) async-start(bf16[8,128,672]{1,2,0:T(8,128)(2,1)} %fusion.18), calls=%async_computation | async-start | bytes 2752512 | tf_op jit(solution)/shard_map/all_to_all | solution.py:141
Sparse Core Ops, SparseCore 0:
  343.7 50.8 reduce-scatter.1
